TPU v7x, 256 devices: a whole 4x4x8 slice. The times are simulated.
256 devices in a mesh: dp: 16 (over x, y), head: 16 (over z, core).
Axes of the slice: x: 4, y: 4, z: 8, core: 2. Of those that a mesh axis runs over, the one named last changes fastest.
Arguments:
- query: bfloat16 [32768, 12288], P(('dp', 'head')), may hold values from -160 to 160
- latent: bfloat16 [32768, 576], P(('dp', 'head')), may hold values from -6 to 6
- d_attn: bfloat16 [32768, 8192], P(('dp', 'head')), may hold values from -6 to 6
- w_kv: bfloat16 [512, 16384], P('dp', 'head'), may hold values from -0.25 to 0.25
- doc_lengths: int32 [16, 10], P('dp'), may hold values from 1 to 384, 2048 in all within a row
Outputs:
- d_query: bfloat16 [32768, 12288], P(('dp', 'head'))
- d_latent: float32 [32768, 576], P(('dp', 'head'))
- d_w_kv: float32 [512, 16384], P('dp', 'head')
Inputs may be any that keep to these rules, and one draw needn't show every extreme that they name: `doc_lengths`: row g lists the lengths of the 10 documents of data group g; they sum to 2048, and the longest of each row is exactly 384.
All inputs are finite; a program needn't handle non-finite values.
Results may differ from a plain program's by a relative error of at most 0.025.
Values may be sent and summed in bfloat16 or wider, within the bound.
No kernel may reach another device: no remote copies, remote signals or barrier semaphores. Data moves between devices by JAX's collectives and lax.ppermute only.
A program may use at most 128 MiB of HBM per device.

v0:
```python
import math
import jax
import jax.numpy as jnp
from jax import lax
from jax.sharding import PartitionSpec as P

NOPE = 128
ROPE = 64
VDIM = 128
KV_RANK = 512
DOC_MAX = 384
QB = 128
masked_score = -1e30


def document_index(lengths_row, count):
    ends = jnp.cumsum(lengths_row)
    positions = jnp.arange(count, dtype=jnp.int32)
    return jnp.sum((positions[:, None] >= ends[None, :]).astype(jnp.int32), axis=1)


def attend_backward(queries, keys_padded, values_padded, grads_out, doc_padded, block, window):
    seq_len = queries.shape[0]
    reach = window - block
    scale = 1.0 / math.sqrt(queries.shape[2])
    blocks = seq_len // block

    def one_block(carry, index):
        grad_keys, grad_values = carry
        first = index * block
        query_rows = lax.dynamic_slice_in_dim(queries, first, block, 0)
        key_rows = lax.dynamic_slice_in_dim(keys_padded, first, window, 0)
        value_rows = lax.dynamic_slice_in_dim(values_padded, first, window, 0)
        out_rows = lax.dynamic_slice_in_dim(grads_out, first, block, 0)
        query_doc = lax.dynamic_slice_in_dim(doc_padded, first + reach, block, 0)
        key_doc = lax.dynamic_slice_in_dim(doc_padded, first, window, 0)
        query_pos = jnp.arange(block, dtype=jnp.int32) + reach
        key_pos = jnp.arange(window, dtype=jnp.int32)
        allowed = (key_pos[None, :] <= query_pos[:, None]) & (
            key_doc[None, :] == query_doc[:, None]
        )
        scores = (
            jnp.einsum("qhd,khd->hqk", query_rows, key_rows, preferred_element_type=jnp.float32)
            * scale
        )
        scores = jnp.where(allowed[None], scores, masked_score)
        top = jnp.max(scores, axis=2, keepdims=True)
        weights = jnp.exp(scores - top)
        probs = weights / jnp.sum(weights, axis=2, keepdims=True)
        probs_low = probs.astype(jnp.bfloat16)
        attn_out = jnp.einsum(
            "hqk,khd->qhd", probs_low, value_rows, preferred_element_type=jnp.float32
        )
        delta = jnp.sum(out_rows.astype(jnp.float32) * attn_out, axis=2)
        dprob = jnp.einsum("qhd,khd->hqk", out_rows, value_rows, preferred_element_type=jnp.float32)
        dscore_low = (probs * (dprob - jnp.transpose(delta)[:, :, None])).astype(jnp.bfloat16)
        grad_query = (
            jnp.einsum("hqk,khd->qhd", dscore_low, key_rows, preferred_element_type=jnp.float32)
            * scale
        )
        grad_key_rows = (
            jnp.einsum("hqk,qhd->khd", dscore_low, query_rows, preferred_element_type=jnp.float32)
            * scale
        )
        grad_value_rows = jnp.einsum(
            "hqk,qhd->khd", probs_low, out_rows, preferred_element_type=jnp.float32
        )
        grad_keys = lax.dynamic_update_slice_in_dim(
            grad_keys,
            lax.dynamic_slice_in_dim(grad_keys, first, window, 0) + grad_key_rows,
            first,
            0,
        )
        grad_values = lax.dynamic_update_slice_in_dim(
            grad_values,
            lax.dynamic_slice_in_dim(grad_values, first, window, 0) + grad_value_rows,
            first,
            0,
        )
        return ((grad_keys, grad_values), grad_query.astype(jnp.bfloat16))

    start_keys = jnp.zeros(keys_padded.shape, jnp.float32)
    start_values = jnp.zeros(values_padded.shape, jnp.float32)
    (grad_keys, grad_values), grad_queries = lax.scan(
        one_block, (start_keys, start_values), jnp.arange(blocks, dtype=jnp.int32)
    )
    grad_queries = grad_queries.reshape(seq_len, queries.shape[1] * queries.shape[2])
    return (grad_keys[reach:], grad_values[reach:], grad_queries)


def local(query, latent, d_attn, w_kv, doc_lengths):
    group_size = lax.axis_size("head")
    own_tokens = query.shape[0]
    seq_len = own_tokens * group_size
    head_count = w_kv.shape[1] // (NOPE + VDIM)
    queries, grads_out = (
        lax.all_to_all(query, "head", split_axis=1, concat_axis=0, tiled=True),
        lax.all_to_all(d_attn, "head", split_axis=1, concat_axis=0, tiled=True),
    )
    latents = lax.all_gather(latent, "head", axis=0, tiled=True)
    compressed = latents[:, :KV_RANK]
    whole_weight = lax.all_gather(w_kv, "dp", axis=0, tiled=True)
    kv_up = jnp.dot(compressed, whole_weight, preferred_element_type=jnp.float32)
    kv_up = kv_up.astype(jnp.bfloat16).reshape(seq_len, head_count, NOPE + VDIM)
    rotary = jnp.broadcast_to(latents[:, None, KV_RANK:], (seq_len, head_count, ROPE))
    keys = jnp.concatenate([kv_up[:, :, :NOPE], rotary], axis=2)
    keys_padded = jnp.concatenate(
        [jnp.zeros((DOC_MAX, head_count, NOPE + ROPE), jnp.bfloat16), keys], axis=0
    )
    values_padded = jnp.concatenate(
        [jnp.zeros((DOC_MAX, head_count, VDIM), jnp.bfloat16), kv_up[:, :, NOPE:]], axis=0
    )
    doc_ids = document_index(doc_lengths[0], seq_len)
    doc_padded = jnp.concatenate([jnp.full((DOC_MAX,), -1, jnp.int32), doc_ids])
    grad_keys, grad_values, grad_queries = attend_backward(
        queries.reshape(seq_len, head_count, NOPE + ROPE),
        keys_padded,
        values_padded,
        grads_out.reshape(seq_len, head_count, VDIM),
        doc_padded,
        QB,
        DOC_MAX + QB,
    )
    returned = lax.all_to_all(grad_queries, "head", split_axis=0, concat_axis=1, tiled=True)
    grad_kv = jnp.concatenate([grad_keys[:, :, :NOPE], grad_values], axis=2).astype(jnp.bfloat16)
    grad_kv = grad_kv.reshape(seq_len, head_count * (NOPE + VDIM))
    grad_weight = lax.psum_scatter(
        lax.dot_general(
            compressed, grad_kv, (((0,), (0,)), ((), ())), preferred_element_type=jnp.float32
        ).astype(jnp.bfloat16),
        "dp",
        scatter_dimension=0,
        tiled=True,
    ).astype(jnp.float32)
    grad_compressed = lax.dot_general(
        grad_kv, whole_weight, (((1,), (1,)), ((), ())), preferred_element_type=jnp.float32
    )
    head_terms = jnp.concatenate([grad_compressed, jnp.sum(grad_keys[:, :, NOPE:], axis=1)], axis=1)
    summed = lax.psum(head_terms.astype(jnp.bfloat16), "head").astype(jnp.float32)
    grad_latent = lax.dynamic_slice_in_dim(
        summed, lax.axis_index("head") * own_tokens, own_tokens, 0
    )
    return (returned, grad_latent, grad_weight)


def solution(mesh):
    placed = (
        P(("dp", "head"), None),
        P(("dp", "head"), None),
        P(("dp", "head"), None),
        P("dp", "head"),
        P("dp", None),
    )
    return jax.shard_map(
        local,
        mesh=mesh,
        in_specs=placed,
        out_specs=(P(("dp", "head"), None), P(("dp", "head"), None), P("dp", "head")),
        check_vma=False,
    )
```

profile of v0, /device:TPU:2, one launch (start us, length us, event | category | flops | bytes accessed | tf_op | source)
XLA Modules:
  0.0 728.3 jit_solution(18205139117940249030)
XLA Ops:
  7.2 4.1 copy.52
  11.2 8.6 %all-to-all-start.1 = ((bf16[128,16,512]{0,2,1:T(8,128)(2,1)}), bf16[128,16,512]{0,2,1:T(8,128)(2,1)S(1)}, u32[]{:S(2)}, u32[]{:S(2)}) async-start(bf16[128,16,512]{0,2,1:T(8,128)(2,1)} %bitcast.74), calls=%async_computation.1 | async-start | bytes 4194304 | tf_op jit(solution)/shard_map/all_to_all | solution.py:98
  21.3 4.6 copy.50
  25.9 43.1 %all-to-all-done.1 = bf16[128,16,512]{0,2,1:T(8,128)(2,1)S(1)} async-done(((bf16[128,16,512]{0,2,1:T(8,128)(2,1)}), bf16[128,16,512]{0,2,1:T(8,128)(2,1)S(1)}, u32[]{:S(2)}, u32[]{:S(2)}) %all-to-all-start.1) | async-done | bytes 2097184 | tf_op jit(solution)/shard_map/all_to_all | solution.py:98
  70.4 4.7 all-to-all-start
  75.4 4.3 copy.53
  79.7 4.2 reshape.117
  83.9 74.2 %all-gather.3.cloned.1.call-done = bf16[2048,576]{0,1:T(8,128)(2,1)} async-done(((bf16[128,576]{0,1:T(8,128)(2,1)}), bf16[2048,576]{0,1:T(8,128)(2,1)}) %all-gather.3.cloned.1.call-update) | async-done | bytes 2359312 | tf_op jit(solution)/shard_map/all_gather | solution.py:100
  158.1 4.2 convolution_convert_fusion
  165.0 4.0 copy.66
  168.9 3.4 concatenate.23
  174.4 3.7 copy.51
  178.1 5.8 reshape.113
  183.9 3.5 broadcast_in_dim.54
  190.0 266.0 %while.16 = (s32[]{:T(128)}, f32[2432,4,192]{0,2,1:T(8,128)}, f32[2432,4,128]{0,2,1:T(8,128)}, bf16[16,128,4,192]{1,3,2,0:T(8,128)(2,1)}, s32[16]{0:T(128)S(1)},...) while((s32[]{:T(128)}, f32[2432,4,192]{0,2,1:T(8,128)}, ...), condition=%wide.region_6.7_spmd, body=%wide.region_2.6_spmd.sunk | while | flops 711002240 | bytes 15294786 | solution.py:84
  201.1 3.3 fusion.128
  234.4 3.3 fusion.128
  251.0 3.3 fusion.128
  267.7 3.3 fusion.128
  300.9 3.3 fusion.128
  317.5 3.3 fusion.128
  334.1 3.3 fusion.128
  367.3 3.3 fusion.128
  384.0 3.3 fusion.128
  417.2 3.3 fusion.128
  433.8 3.3 fusion.128
  455.9 4.7 copy.56
  460.6 6.1 all-to-all-start.2
  479.1 6.3 fusion.67
  487.7 142.7 %all-reduce.5.cloned.1.call-done = bf16[2048,576]{0,1:T(8,128)(2,1)} async-done(((bf16[2048,576]{0,1:T(8,128)(2,1)}), bf16[2048,576]{0,1:T(8,128)(2,1)}) %all-reduce.5.cloned.1.call-update) | async-done | bytes 2359312 | tf_op jit(solution)/shard_map/psum | solution.py:139
  632.0 80.5 %reduce-scatter.4.cloned.1.call-done = bf16[32,1024]{1,0:T(8,128)(2,1)} async-done(((bf16[512,1024]{1,0:T(8,128)(2,1)}), bf16[32,1024]{1,0:T(8,128)(2,1)}) %reduce-scatter.4.cloned.1.call-update) | async-done | bytes 65552
  717.1 4.6 copy.58
  (240 shorter events, 249.7 us)
Async XLA Ops:
  11.2 57.8 %all-to-all-start.1 = ((bf16[128,16,512]{0,2,1:T(8,128)(2,1)}), bf16[128,16,512]{0,2,1:T(8,128)(2,1)S(1)}, u32[]{:S(2)}, u32[]{:S(2)}) async-start(bf16[128,16,512]{0,2,1:T(8,128)(2,1)} %bitcast.74), calls=%async_computation.1 | async-start | bytes 4194304 | tf_op jit(solution)/shard_map/all_to_all | solution.py:98
  19.8 64.1 %all-gather.5.cloned.1.call-start = ((), (), s32[]{:S(2)}) async-start(), calls=%async_computation.5 | async-start | bytes 1114112 | tf_op jit(solution)/shard_map/all_gather | solution.py:102
  20.6 137.6 %all-gather.3.cloned.1.call-start = ((), (), s32[]{:S(2)}) async-start(), calls=%async_computation.4 | async-start | bytes 2506752 | tf_op jit(solution)/shard_map/all_gather | solution.py:100
  69.0 1.4 copy-start
  69.0 6.0 copy-start.4
  70.4 104.0 %all-to-all-start = ((bf16[128,16,768]{0,2,1:T(8,128)(2,1)}), bf16[128,16,768]{0,2,1:T(8,128)(2,1)S(1)}, u32[]{:S(2)}, u32[]{:S(2)}) async-start(bf16[128,16,768]{0,2,1:T(8,128)(2,1)} %bitcast.7), calls=%async_computation | async-start | bytes 6291456 | tf_op jit(solution)/shard_map/all_to_all | solution.py:97
  168.9 3.4 slice-start
  168.9 3.5 copy-start.1
  460.6 253.7 %all-to-all-start.2 = ((bf16[16,128,768]{2,1,0:T(8,128)(2,1)}), bf16[16,128,768]{2,1,0:T(8,128)(2,1)S(1)}, u32[]{:S(2)}, u32[]{:S(2)}) async-start(bf16[16,128,768]{2,1,0:T(8,128)(2,1)} %copy.56), calls=%async_computation.2 | async-start | bytes 6291456 | tf_op jit(solution)/shard_map/all_to_all | solution.py:124
  466.7 163.7 %all-reduce.5.cloned.1.call-start = ((), (), s32[]{:S(2)}) async-start(), calls=%async_computation.6 | async-start | bytes 4718592 | tf_op jit(solution)/shard_map/psum | solution.py:139
  473.7 1.2 copy-start.3
  474.3 3.0 copy-start.2
  479.0 233.5 %reduce-scatter.4.cloned.1.call-start = ((), (), s32[]{:S(2)}) async-start(), calls=%async_computation.7 | async-start | bytes 1114112
Sparse Core Ops, SparseCore 0:
  23.1 48.6 all-gather.4
  73.5 84.6 all-gather.2
  479.2 151.1 all-reduce.4
  633.7 78.7 reduce-scatter.3
where the time goes:
time: 733 us; the launch traced here: 728 us
  waiting for transfers between devices  342 us (47%)
  matrix products  237 us (32%)
  local copies, waits for them, and re-layouts  94.5 us (13%)
  starting transfers between devices  19.7 us (3%)
  between operations  13.9 us (2%)
  loops' own time  11.1 us (2%)
  other arithmetic  10.1 us (1%)
    psum x1, waiting for transfers between devices, local(): lax.psum(head_terms.astype(jnp.bfloat16), 'head').astype(jnp.float32)  143 us
    unnamed x5, waiting for transfers between devices  81.9 us
    all_gather x1, waiting for transfers between devices, local(): latents = lax.all_gather(latent, 'head', axis=0, tiled=True)  74.2 us
    dot_general x16, matrix products, one_block(): jnp.einsum('hqk,qhd->khd', probs_low, out_rows, preferred_element_type=jn...  52.8 us
    dot_general x16, matrix products, one_block(): jnp.einsum('hqk,qhd->khd', dscore_low, query_rows, preferred_element_type...  49.7 us
    all_to_all x1, waiting for transfers between devices, local(): lax.all_to_all(d_attn, 'head', split_axis=1, concat_axis=0, tiled=True)  43.1 us
    dot_general x16, matrix products, one_block(): jnp.einsum('hqk,khd->qhd', dscore_low, key_rows, preferred_element_type=j...  34.8 us
    dot_general x16, matrix products, one_block(): jnp.einsum('hqk,khd->qhd', probs_low, value_rows, preferred_element_type=...  34.8 us
  transfers between devices with their start and end apart: 7, of which 4 were waited for; matrix products, arithmetic and copies ran while one was open for 7% of the time, Pallas kernels for 0%

commit v1 on v0

--- a/solution.py
+++ b/solution.py
@@ -97,7 +97,9 @@
         lax.all_to_all(query, "head", split_axis=1, concat_axis=0, tiled=True),
         lax.all_to_all(d_attn, "head", split_axis=1, concat_axis=0, tiled=True),
     )
-    latents = lax.all_gather(latent, "head", axis=0, tiled=True)
+    latents = jnp.concatenate(
+        lax.all_to_all(jnp.stack([latent] * lax.axis_size("head")), "head", 0, 0), axis=0
+    )
     compressed = latents[:, :KV_RANK]
     whole_weight = lax.all_gather(w_kv, "dp", axis=0, tiled=True)
     kv_up = jnp.dot(compressed, whole_weight, preferred_element_type=jnp.float32)

time: 733 us -> 765 us (1.044)
  blocking collectives: 0 us -> 58.3 us
  waiting for transfers between devices: 342 us -> 317 us
    all_gather x1 -> x0, waiting for transfers between devices: 74.2 us -> none  [local(): latents = lax.all_gather(latent, 'head', axis=0, tiled=True)]
    all_to_all x0 -> x1, blocking collectives: none -> 58.3 us  [local(): lax.all_to_all(d_attn, 'head', split_axis=1, concat_axis=0, tiled=True)]
    all_gather x1, waiting for transfers between devices: 0.01 us -> 38.8 us  [local(): whole_weight = lax.all_gather(w_kv, 'dp', axis=0, tiled=True)]
    unnamed x17 -> x21, local copies, waits for them, and re-layouts: 23.4 us -> 24 us
    unnamed x5 -> x4, waiting for transfers between devices: 81.9 us -> 81.5 us
  transfers between devices with their start and end apart: 7 -> 6, of which waited for: 4 -> 5; matrix products, arithmetic and copies ran while one was open for 7% -> 7% of each run, Pallas kernels for 0% -> 0%
where the time goes in v1:
time: 765 us; the launch traced here: 760 us
  waiting for transfers between devices  317 us (41%)
  matrix products  237 us (31%)
  local copies, waits for them, and re-layouts  99.1 us (13%)
  blocking collectives  58.3 us (8%)
  between operations  13.9 us (2%)
  starting transfers between devices  13.8 us (2%)
  loops' own time  11.1 us (1%)
  other arithmetic  10.1 us (1%)
    psum x1, waiting for transfers between devices, local(): lax.psum(head_terms.astype(jnp.bfloat16), 'head').astype(jnp.float32)  143 us
    unnamed x4, waiting for transfers between devices  81.5 us
    all_to_all x1, blocking collectives, local(): lax.all_to_all(d_attn, 'head', split_axis=1, concat_axis=0, tiled=True)  58.3 us
    dot_general x16, matrix products, one_block(): jnp.einsum('hqk,qhd->khd', probs_low, out_rows, preferred_element_type=jn...  52.8 us
    all_to_all x1, waiting for transfers between devices, local(): lax.all_to_all(jnp.stack([latent] * lax.axis_size('head')), 'head', 0, 0)  50.2 us
    dot_general x16, matrix products, one_block(): jnp.einsum('hqk,qhd->khd', dscore_low, query_rows, preferred_element_type...  49.7 us
    all_gather x1, waiting for transfers between devices, local(): whole_weight = lax.all_gather(w_kv, 'dp', axis=0, tiled=True)  38.8 us
    dot_general x16, matrix products, one_block(): jnp.einsum('hqk,khd->qhd', dscore_low, key_rows, preferred_element_type=j...  34.8 us
  transfers between devices with their start and end apart: 6, of which 5 were waited for; matrix products, arithmetic and copies ran while one was open for 7% of the time, Pallas kernels for 0%

profile of v1, /device:TPU:2, one launch (start us, length us, event | category | flops | bytes accessed | tf_op | source)
XLA Modules:
  0.0 760.2 jit_solution(4930533409590585234)
XLA Ops:
  10.4 58.3 %all_to_all.56 = bf16[128,16,512]{0,2,1:T(8,128)(2,1)} all-to-all(bf16[128,16,512]{0,2,1:T(8,128)(2,1)S(1)} %bitcast.79), channel_id=1, replica_groups=mesh['dp'=16,'head'=16] {'head'}, dimensions={1} | all-to-all | bytes 4194304 | tf_op jit(solution)/shard_map/all_to_all | solution.py:98
  70.5 4.2 all-to-all-start.1
  74.8 4.6 copy.51
  79.4 50.2 %all-to-all-done.1 = bf16[16,128,576]{1,2,0:T(8,128)(2,1)S(1)} async-done(((bf16[16,128,576]{1,2,0:T(8,128)(2,1)}), bf16[16,128,576]{1,2,0:T(8,128)(2,1)S(1)}, u32[]{:S(2)}, u32[]{:S(2)}) %all-to-all-start.1) | async-done | bytes 2359328 | tf_op jit(solution)/shard_map/all_to_all | solution.py:101
  131.1 4.6 all-to-all-start
  136.8 4.3 copy.55
  141.1 4.2 reshape.123
  148.8 38.8 %all-gather.2.cloned.1.call-done = bf16[512,1024]{1,0:T(8,128)(2,1)} async-done(((bf16[32,1024]{1,0:T(8,128)(2,1)}), bf16[512,1024]{1,0:T(8,128)(2,1)}) %all-gather.2.cloned.1.call-update) | async-done | bytes 1048592 | tf_op jit(solution)/shard_map/all_gather | solution.py:104
  187.6 4.2 convolution_convert_fusion
  194.4 4.0 copy.68
  198.4 3.4 concatenate.23
  203.9 3.6 all-to-all-done
  207.5 3.7 copy.52
  211.2 5.8 reshape.118
  217.0 3.5 broadcast_in_dim.54
  223.1 266.0 %while.16 = (s32[]{:T(128)}, f32[2432,4,192]{0,2,1:T(8,128)}, f32[2432,4,128]{0,2,1:T(8,128)}, bf16[16,128,4,192]{1,3,2,0:T(8,128)(2,1)}, s32[16]{0:T(128)S(1)},...) while((s32[]{:T(128)}, f32[2432,4,192]{0,2,1:T(8,128)}, ...), condition=%wide.region_6.7_spmd, body=%wide.region_2.6_spmd.sunk | while | flops 711002240 | bytes 15294786 | solution.py:84
  234.2 3.3 fusion.129
  267.6 3.3 fusion.129
  284.1 3.3 fusion.129
  300.8 3.3 fusion.129
  334.0 3.3 fusion.129
  350.6 3.3 fusion.129
  367.2 3.3 fusion.129
  417.1 3.3 fusion.129
  450.3 3.3 fusion.129
  467.0 3.3 fusion.129
  489.0 4.7 copy.58
  493.7 4.8 all-to-all-start.3
  510.7 6.3 fusion.67
  519.3 142.8 %all-reduce.5.cloned.1.call-done = bf16[2048,576]{0,1:T(8,128)(2,1)} async-done(((bf16[2048,576]{0,1:T(8,128)(2,1)}), bf16[2048,576]{0,1:T(8,128)(2,1)}) %all-reduce.5.cloned.1.call-update) | async-done | bytes 2359312 | tf_op jit(solution)/shard_map/psum | solution.py:141
  663.7 80.8 %reduce-scatter.4.cloned.1.call-done = bf16[32,1024]{1,0:T(8,128)(2,1)} async-done(((bf16[512,1024]{1,0:T(8,128)(2,1)}), bf16[32,1024]{1,0:T(8,128)(2,1)}) %reduce-scatter.4.cloned.1.call-update) | async-done | bytes 65552
  749.1 4.6 copy.60
  (244 shorter events, 260.6 us)
Async XLA Ops:
  10.4 58.3 %copy-start.4 = (bf16[128,576]{0,1:T(8,128)(2,1)S(1)}, bf16[128,576]{0,1:T(8,128)(2,1)}, u32[]{:S(2)}) copy-start(bf16[128,576]{0,1:T(8,128)(2,1)} %param.8) | copy-start | bytes 442372
  70.5 59.1 %all-to-all-start.1 = ((bf16[16,128,576]{1,2,0:T(8,128)(2,1)}), bf16[16,128,576]{1,2,0:T(8,128)(2,1)S(1)}, u32[]{:S(2)}, u32[]{:S(2)}) async-start(bf16[16,128,576]{1,2,0:T(8,128)(2,1)} %stack.2), calls=%async_computation.1 | async-start | bytes 4718592 | tf_op jit(solution)/shard_map/all_to_all | solution.py:101
  129.6 1.4 copy-start
  129.6 6.8 copy-start.6
  131.1 76.5 %all-to-all-start = ((bf16[128,16,768]{0,2,1:T(8,128)(2,1)}), bf16[128,16,768]{0,2,1:T(8,128)(2,1)S(1)}, u32[]{:S(2)}, u32[]{:S(2)}) async-start(bf16[128,16,768]{0,2,1:T(8,128)(2,1)} %bitcast.7), calls=%async_computation | async-start | bytes 6291456 | tf_op jit(solution)/shard_map/all_to_all | solution.py:97
  135.7 51.9 %all-gather.2.cloned.1.call-start = ((), (), s32[]{:S(2)}) async-start(), calls=%async_computation.5 | async-start | bytes 1114112 | tf_op jit(solution)/shard_map/all_gather | solution.py:104
  147.3 1.4 copy-start.3
  198.4 3.4 slice-start
  198.4 3.5 copy-start.1
  493.7 252.6 %all-to-all-start.3 = ((bf16[16,128,768]{2,1,0:T(8,128)(2,1)}), bf16[16,128,768]{2,1,0:T(8,128)(2,1)S(1)}, u32[]{:S(2)}, u32[]{:S(2)}) async-start(bf16[16,128,768]{2,1,0:T(8,128)(2,1)} %copy.58), calls=%async_computation.3 | async-start | bytes 6291456 | tf_op jit(solution)/shard_map/all_to_all | solution.py:126
  498.5 163.6 %all-reduce.5.cloned.1.call-start = ((), (), s32[]{:S(2)}) async-start(), calls=%async_computation.6 | async-start | bytes 4718592 | tf_op jit(solution)/shard_map/psum | solution.py:141
  505.3 1.2 copy-start.5
  505.9 3.0 copy-start.2
  510.6 233.8 %reduce-scatter.4.cloned.1.call-start = ((), (), s32[]{:S(2)}) async-start(), calls=%async_computation.7 | async-start | bytes 1114112
Sparse Core Ops, SparseCore 0:
  139.0 48.6 all-gather.1
  510.8 151.2 all-reduce.4
  665.6 78.8 reduce-scatter.3
